TPU v7x, 512 devices: a whole 4x8x8 slice. The times are simulated.
512 devices in a mesh: head: 8 (over z), tok: 64 (over x, y, core).
Axes of the slice: x: 4, y: 8, z: 8, core: 2. Of those that a mesh axis runs over, the one named last changes fastest.
Arguments:
- patches: bfloat16 [32768, 1280], P('tok')
- row_table: bfloat16 [64, 1280], replicated, may hold values from -0.59765625 to 0.59765625
- col_table: bfloat16 [64, 1280], replicated, may hold values from -0.59765625 to 0.59765625
- qkv_weight: bfloat16 [3, 1280, 1280], P(None, 'head'), may hold values from -0.15625 to 0.15625
- out_weight: bfloat16 [1280, 1280], P('head'), may hold values from -0.15625 to 0.15625
- merge_weight: bfloat16 [1280, 5120], P('head'), may hold values from -0.078125 to 0.078125
- segment_ids: int32 [32768], P('tok'), may hold values from 0 to 63, as said below
- image_grids: int32 [64, 2], replicated, may hold values from 2 to 62, as said below
- image_offsets: int32 [64], replicated, may hold values from 0 to 32736, as said below
- owners: int32 [64], replicated, may hold values from 0 to 63, each once
Outputs:
- delivered: bfloat16 [15872, 1280], P('tok', 'head')
Inputs may be any that keep to these rules, and one draw needn't show every extreme that they name: `segment_ids`: tokens of each image are consecutive and images follow in order; the pair p of token blocks (tokens 2 * p * 512 to 2 * (p + 1) * 512 - 1) holds exactly images 2 * p and 2 * p + 1, with no padding. `image_grids`: heights are even, widths are 16, and height times width is the image's token count. Within an image each 2x2 window of patches is four consecutive tokens (top left, top right, bottom left, bottom right), windows in row-major order. The longest image has exactly 992 tokens. `image_offsets`: the first token of each image, consistent with segment_ids. `owners`: every device index along tok owns exactly one image.
All inputs are finite; a program needn't handle non-finite values.
Results may differ from a plain program's by a relative error of at most 0.019.
Values may be sent and summed in bfloat16 or wider, within the bound.
No kernel may reach another device: no remote copies, remote signals or barrier semaphores. Data moves between devices by JAX's collectives and lax.ppermute only.
A program may use at most 64 MiB of HBM per device.

v0:
```python
import math
import jax
import jax.numpy as jnp
from jax import lax
from jax.sharding import PartitionSpec as P

HEAD_DIM = 80
CAP = 248


def partner(x, axis, apart):
    return lax.ppermute(x, axis, [(i, i ^ 1 << apart) for i in range(lax.axis_size(axis))])


def layer_norm(values):
    centered = values - jnp.mean(values, axis=-1, keepdims=True)
    variance = jnp.mean(centered * centered, axis=-1, keepdims=True)
    return centered * lax.rsqrt(variance + 1e-06)


def grid_place(token_pos, start_tok, width_now):
    local_pos = token_pos - start_tok
    window = local_pos // 4
    quarter = local_pos % 4
    half_width = jnp.maximum(width_now // 2, 1)
    row_index = 2 * (window // half_width) + quarter // 2
    col_index = 2 * (window % half_width) + quarter % 2
    return (row_index, col_index)


def dot_last(left, right):
    return lax.dot_general(
        left, right, (((1,), (1,)), ((), ())), preferred_element_type=jnp.float32
    )


def on_device(
    patches,
    row_table,
    col_table,
    qkv_weight,
    out_weight,
    merge_weight,
    segment_ids,
    image_grids,
    image_offsets,
    owners,
):
    full_weight = lax.all_gather(out_weight, "head", axis=0, tiled=True)
    block_rows = patches.shape[0]
    width_here = qkv_weight.shape[1]
    heads_here = width_here // HEAD_DIM
    image_count = owners.shape[0]
    image_ids = jnp.arange(image_count, dtype=jnp.int32)
    token_pos = lax.axis_index("tok") * block_rows + jnp.arange(block_rows, dtype=jnp.int32)
    member = segment_ids[:, None] == image_ids[None, :]
    start_tok = jnp.sum(jnp.where(member, image_offsets[None, :], 0), axis=1)
    width_now = jnp.sum(jnp.where(member, image_grids[None, :, 1], 0), axis=1)
    row_index, col_index = grid_place(token_pos, start_tok, width_now)
    side_ids = jnp.arange(row_table.shape[0], dtype=jnp.int32)
    row_onehot = (row_index[:, None] == side_ids[None, :]).astype(jnp.bfloat16)
    col_onehot = (col_index[:, None] == side_ids[None, :]).astype(jnp.bfloat16)
    resid = (
        patches.astype(jnp.float32)
        + jnp.dot(row_onehot, row_table, preferred_element_type=jnp.float32)
        + jnp.dot(col_onehot, col_table, preferred_element_type=jnp.float32)
    )
    normed = layer_norm(resid).astype(jnp.bfloat16)
    query_rows = dot_last(normed, qkv_weight[0]).astype(jnp.bfloat16)
    key_rows = dot_last(normed, qkv_weight[1]).astype(jnp.bfloat16)
    value_rows = dot_last(normed, qkv_weight[2]).astype(jnp.bfloat16)
    seg_wire = segment_ids.astype(jnp.bfloat16)
    far_keys, far_values, far_seg = partner((key_rows, value_rows, seg_wire), "tok", 0)
    query_heads = query_rows.reshape(block_rows, heads_here, HEAD_DIM)
    key_heads = jnp.concatenate([key_rows, far_keys], axis=0).reshape(
        2 * block_rows, heads_here, HEAD_DIM
    )
    value_heads = jnp.concatenate([value_rows, far_values], axis=0).reshape(
        2 * block_rows, heads_here, HEAD_DIM
    )
    query_seg = seg_wire.astype(jnp.float32)
    key_seg = jnp.concatenate([seg_wire, far_seg], axis=0).astype(jnp.float32)
    scores = jnp.einsum(
        "qhd,khd->hqk", query_heads, key_heads, preferred_element_type=jnp.float32
    ) * (1.0 / math.sqrt(HEAD_DIM))
    same_image = query_seg[:, None] == key_seg[None, :]
    raw_weights = jnp.where(same_image[None], jnp.exp(scores), 0.0)
    weight_sum = jnp.sum(raw_weights, axis=-1, keepdims=True)
    attn_probs = (raw_weights / weight_sum).astype(jnp.bfloat16)
    mixed = jnp.einsum("hqk,khd->qhd", attn_probs, value_heads, preferred_element_type=jnp.float32)
    attended = mixed.reshape(block_rows, width_here).astype(jnp.bfloat16)
    group = lax.axis_size("head")
    sent = jnp.broadcast_to(attended[None], (group,) + attended.shape)
    gathered = lax.all_to_all(sent, "head", 0, 0, tiled=True)
    head_total = jnp.einsum(
        "ztf,zfd->td",
        gathered,
        full_weight.reshape(group, width_here, -1),
        preferred_element_type=jnp.float32,
    )
    normed_two = layer_norm(resid + head_total).astype(jnp.bfloat16)
    merged = normed_two.reshape(block_rows // 4, 4 * normed_two.shape[1])
    projected = dot_last(merged, merge_weight).astype(jnp.bfloat16)
    places = lax.axis_size("tok")
    rows_here = projected.shape[0]
    share = rows_here // places
    spread = lax.all_to_all(projected.reshape(places, share, width_here), "tok", 0, 0, tiled=True)
    pair_ids = jnp.arange(places // 2, dtype=jnp.int32)
    place_ids = jnp.arange(places, dtype=jnp.int32)
    wanted = (owners.reshape(-1, 2)[None, :, :] == place_ids[:, None, None]).any(axis=2)
    pieces = jnp.dot(
        wanted.astype(jnp.bfloat16),
        spread.reshape(places // 2, 2 * share * width_here),
        preferred_element_type=jnp.float32,
    ).astype(jnp.bfloat16)
    pair_rows = lax.all_to_all(
        pieces.reshape(places, 2 * share, width_here), "tok", 0, 0, tiled=True
    ).reshape(2 * rows_here, width_here)
    owner_mask = owners == lax.axis_index("tok")
    image_id = jnp.sum(jnp.where(owner_mask, image_ids, 0))
    first_row = (
        jnp.sum(jnp.where(owner_mask, image_offsets, 0)) // 4 - image_id // 2 * 2 * rows_here
    )
    merged_count = jnp.sum(jnp.where(owner_mask, image_grids[:, 0] * image_grids[:, 1], 0)) // 4
    slot_ids = jnp.arange(CAP, dtype=jnp.int32)
    got_ids = jnp.arange(2 * rows_here, dtype=jnp.int32)
    row_of = got_ids // share % 2 * rows_here + got_ids // (2 * share) * share + got_ids % share
    slot_of = row_of - first_row
    selector = (slot_of[None, :] == slot_ids[:, None]) & (slot_ids < merged_count)[:, None]
    owner_rows = jnp.dot(
        selector.astype(jnp.bfloat16), pair_rows, preferred_element_type=jnp.float32
    )
    return owner_rows.astype(jnp.bfloat16)


def solution(mesh):
    placed = (
        P("tok", None),
        P(),
        P(),
        P(None, "head", None),
        P("head", None),
        P("head", None),
        P("tok"),
        P(),
        P(),
        P(),
    )
    return jax.shard_map(
        on_device, mesh=mesh, in_specs=placed, out_specs=P("tok", "head"), check_vma=False
    )
```

profile of v0, /device:TPU:1, one launch (start us, length us, event | category | flops | bytes accessed | tf_op | source)
XLA Modules:
  0.0 146.8 jit_solution(14957617930545872145)
XLA Ops:
  6.5 0.0 copy-start
  6.5 0.0 copy-start.2
  6.5 0.0 all-gather.2.cloned.1.call-start
  6.5 0.7 all-gather.2.cloned.1.call-update
  7.3 0.7 slice_bitcast_fusion
  7.9 0.8 select_reduce_fusion
  8.7 0.1 fusion.22
  8.9 2.0 %convolution_add_fusion.1 = f32[512,1280]{1,0:T(8,128)S(1)} fusion(bf16[64,1280]{1,0:T(8,128)(2,1)} %param.11, bf16[512,1280]{1,0:T(8,128)(2,1)} %param.10, s32[512]{0:T(512)S(1)} %get-tuple-element.13), kind=kOutput, calls=%fused_computation.3 | convolution fusion | flops 85229568 | bytes 4098048 | tf_op jit(solution)/shard_map/dot_general | solution.py:65
  10.9 0.0 copy-done.2
  10.9 0.6 fusion.41
  11.5 0.0 copy-start.1
  11.5 0.4 multiply_reduce_fusion.1
  11.9 0.0 copy-start.7
  11.9 0.0 copy-start.3
  12.0 0.3 multiply_convert_fusion.1
  12.3 0.8 copy-done.1
  13.0 0.7 copy-done.7
  13.7 0.6 convolution_convert_fusion
  14.3 8.8 %collective-permute-start.2 = (bf16[512,160]{0,1:T(8,128)(2,1)S(1)}, bf16[512,160]{0,1:T(8,128)(2,1)S(1)}, u32[]{:S(2)}, u32[]{:S(2)}) collective-permute-start(bf16[512,160]{0,1:T(8,128)(2,1)S(1)} %convolution_convert_fusion), channel_id=1, source_target_pairs={{0,1},{1,0},{2,3},{3,2},{4,5},{5,4},{6,7},{7,6},{8,9},{9,8},{10,11... | collective-permute-start | bytes 491528 | tf_op jit(solution)/shard_map/ppermute | solution.py:12
  23.1 0.0 copy-done.3
  23.1 1.9 %collective-permute-start.1 = (bf16[512]{0:T(512)(128)(2,1)S(1)}, bf16[512]{0:T(512)(128)(2,1)S(1)}, u32[]{:S(2)}, u32[]{:S(2)}) collective-permute-start(bf16[512]{0:T(512)(128)(2,1)S(1)} %get-tuple-element.11), channel_id=1, source_target_pairs={{0,1},{1,0},{2,3},{3,2},{4,5},{5,4},{6,7},{7,6},{8,9},{9,8},{10,11... | collective-permute-start | bytes 3080 | tf_op jit(solution)/shard_map/ppermute | solution.py:12
  25.0 0.6 convolution_convert_fusion.2
  25.6 2.4 %collective-permute-start = (bf16[512,160]{0,1:T(8,128)(2,1)S(1)}, bf16[512,160]{0,1:T(8,128)(2,1)S(1)}, u32[]{:S(2)}, u32[]{:S(2)}) collective-permute-start(bf16[512,160]{0,1:T(8,128)(2,1)S(1)} %convolution_convert_fusion.2), channel_id=1, source_target_pairs={{0,1},{1,0},{2,3},{3,2},{4,5},{5,4},{6,7},{7,6},{8,9},{9,8},{10,11... | collective-permute-start | bytes 491528 | tf_op jit(solution)/shard_map/ppermute | solution.py:12
  28.0 0.6 convolution_convert_fusion.1
  28.6 0.0 collective-permute-done.1
  28.6 0.4 broadcast_compare_fusion
  29.0 0.0 collective-permute-done.2
  29.1 0.0 collective-permute-done
  29.1 1.5 %fusion = (f32[2,512]{1,0:T(2,128)S(1)}, f32[2,512,1024]{2,1,0:T(8,128)S(1)}) fusion(pred[512,1024]{1,0:T(8,128)(4,1)S(1)} %broadcast_compare_fusion, bf16[512,2,80]{0,2,1:T(8,128)(2,1)S(1)} %bitcast.49, bf16[1024,2,80]{0,2,1:T(8,128)(2,1)S(1)} %bitcast.46), kind=kOutput, calls=%fused_computation.4 | convolution fusion | flops 170916864 | bytes 5214208 | tf_op jit(solution)/shard_map/qhd,khd->hqk/dot_general | solution.py:83
  30.6 1.4 fusion.3
  31.9 0.0 copy-start.5
  32.0 0.0 copy-start.4
  32.0 0.0 copy-start.6
  32.0 1.2 broadcast_in_dim.69
  33.2 4.7 %all-to-all-start = ((bf16[8,512,160]{1,2,0:T(8,128)(2,1)}), bf16[8,512,160]{1,2,0:T(8,128)(2,1)S(1)}, u32[]{:S(2)}, u32[]{:S(2)}) async-start(bf16[8,512,160]{1,2,0:T(8,128)(2,1)} %broadcast_in_dim.69), calls=%async_computation | async-start | bytes 2621440 | tf_op jit(solution)/shard_map/all_to_all | solution.py:94
  37.8 0.0 copy-done.5
  37.8 0.1 eq.109
  37.9 0.0 copy-done.4
  38.0 0.0 copy-done.6
  38.0 0.7 fusion.37
  40.0 0.1 copy.12
  41.4 44.9 %all-to-all-done = bf16[8,512,160]{1,2,0:T(8,128)(2,1)S(1)} async-done(((bf16[8,512,160]{1,2,0:T(8,128)(2,1)}), bf16[8,512,160]{1,2,0:T(8,128)(2,1)S(1)}, u32[]{:S(2)}, u32[]{:S(2)}) %all-to-all-start) | async-done | bytes 1310752 | tf_op jit(solution)/shard_map/all_to_all | solution.py:94
  86.3 6.4 %all-gather.2.cloned.1.call-done = bf16[1280,1280]{1,0:T(8,128)(2,1)} async-done(((bf16[160,1280]{1,0:T(8,128)(2,1)}), bf16[1280,1280]{1,0:T(8,128)(2,1)}) %all-gather.2.cloned.1.call-update) | async-done | bytes 3276816 | tf_op jit(solution)/shard_map/all_gather | solution.py:49
  92.7 4.8 %fusion.42 = (f32[512]{0:T(512)S(1)}, f32[512,1280]{1,0:T(8,128)S(1)}) fusion(f32[512,1280]{1,0:T(8,128)} %copy-done.1, bf16[8,512,160]{1,2,0:T(8,128)(2,1)S(1)} %all-to-all-done, bf16[8,160,1280]{2,1,0:T(8,128)(2,1)} %bitcast.45), kind=kOutput, calls=%fused_computation.113 | convolution fusion | flops 1679031808 | bytes 9832448 | tf_op jit(solution)/shard_map/ztf,zfd->td/dot_general | solution.py:95
  97.5 0.4 multiply_reduce_fusion
  98.0 0.3 multiply_convert_fusion
  98.3 1.7 %reshape.260 = bf16[128,5120]{1,0:T(8,128)(2,1)} reshape(bf16[512,1280]{1,0:T(8,128)(2,1)S(1)} %multiply_convert_fusion) | data formatting | bytes 2621440 | tf_op jit(solution)/shard_map/reshape | solution.py:102
  100.0 0.0 copy-done
  100.0 1.9 %convolution_convert_fusion.5 = bf16[128,160]{0,1:T(8,128)(2,1)S(1)} fusion(bf16[128,5120]{1,0:T(8,128)(2,1)} %reshape.260, bf16[160,5120]{1,0:T(8,128)(2,1)S(1)} %copy-done), kind=kOutput, calls=%fused_computation.18 | convolution fusion | flops 209735680 | bytes 2990080 | tf_op jit(solution)/shard_map/dot_general | solution.py:32
  101.9 0.1 copy.13
  102.0 0.7 reshape.261
  102.7 10.4 %all-to-all-start.1 = ((bf16[64,2,160]{2,1,0:T(2,128)(2,1)}), bf16[64,2,160]{2,1,0:T(2,128)(2,1)S(1)}, u32[]{:S(2)}, u32[]{:S(2)}) async-start(bf16[64,2,160]{2,1,0:T(2,128)(2,1)} %reshape.261), calls=%async_computation.1 | async-start | bytes 131072 | tf_op jit(solution)/shard_map/all_to_all | solution.py:107
  113.1 0.1 fusion.16
  113.2 9.7 %all-to-all-done.1 = bf16[64,2,160]{2,1,0:T(2,128)(2,1)S(1)} async-done(((bf16[64,2,160]{2,1,0:T(2,128)(2,1)}), bf16[64,2,160]{2,1,0:T(2,128)(2,1)S(1)}, u32[]{:S(2)}, u32[]{:S(2)}) %all-to-all-start.1) | async-done | bytes 40992 | tf_op jit(solution)/shard_map/all_to_all | solution.py:107
  122.9 0.1 reshape.262
  123.0 0.2 convolution_convert_fusion.4
  123.2 0.8 reshape.263
  124.0 4.4 %all-to-all-start.2 = ((bf16[64,4,160]{2,1,0:T(4,128)(2,1)}), bf16[64,4,160]{2,1,0:T(4,128)(2,1)S(1)}, u32[]{:S(2)}, u32[]{:S(2)}) async-start(bf16[64,4,160]{2,1,0:T(4,128)(2,1)} %reshape.263), calls=%async_computation.2 | async-start | bytes 262144 | tf_op jit(solution)/shard_map/all_to_all | solution.py:116
  133.4 5.5 %all-to-all-done.2 = bf16[64,4,160]{2,1,0:T(4,128)(2,1)S(1)} async-done(((bf16[64,4,160]{2,1,0:T(4,128)(2,1)}), bf16[64,4,160]{2,1,0:T(4,128)(2,1)S(1)}, u32[]{:S(2)}, u32[]{:S(2)}) %all-to-all-start.2) | async-done | bytes 81952 | tf_op jit(solution)/shard_map/all_to_all | solution.py:116
  138.9 0.1 reshape.264
  139.0 0.9 convolution_convert_fusion.3
  (10 shorter events, 0.1 us)
Async XLA Ops:
  6.5 93.4 %copy-start = (bf16[160,5120]{1,0:T(8,128)(2,1)S(1)}, bf16[160,5120]{1,0:T(8,128)(2,1)}, u32[]{:S(2)}) copy-start(bf16[160,5120]{1,0:T(8,128)(2,1)} %param.15) | copy-start | bytes 4915204
  6.5 4.3 %copy-start.2 = (bf16[64,1280]{1,0:T(8,128)(2,1)S(1)}, bf16[64,1280]{1,0:T(8,128)(2,1)}, u32[]{:S(2)}) copy-start(bf16[64,1280]{1,0:T(8,128)(2,1)} %param.12) | copy-start | bytes 491524
  6.5 86.2 %all-gather.2.cloned.1.call-start = ((), (), s32[]{:S(2)}) async-start(), calls=%async_computation.3 | async-start | bytes 3686400 | tf_op jit(solution)/shard_map/all_gather | solution.py:49
  11.5 1.5 %copy-start.1 = (f32[512,1280]{1,0:T(8,128)}, f32[512,1280]{1,0:T(8,128)S(1)}, u32[]{:S(2)}) copy-start(f32[512,1280]{1,0:T(8,128)S(1)} %get-tuple-element.15) | copy-start | bytes 7864324
  11.9 1.8 %copy-start.7 = (bf16[3,160,1280]{2,1,0:T(8,128)(2,1)S(1)}, bf16[3,160,1280]{2,1,0:T(8,128)(2,1)}, u32[]{:S(2)}) copy-start(bf16[3,160,1280]{2,1,0:T(8,128)(2,1)} %param.13) | copy-start | bytes 3686404
  11.9 11.2 %copy-start.3 = (s32[512]{0:T(512)S(1)}, s32[512]{0:T(512)}, u32[]{:S(2)}) copy-start(s32[512]{0:T(512)} %param.16) | copy-start | bytes 6148
  14.3 14.7 %collective-permute-start.2 = (bf16[512,160]{0,1:T(8,128)(2,1)S(1)}, bf16[512,160]{0,1:T(8,128)(2,1)S(1)}, u32[]{:S(2)}, u32[]{:S(2)}) collective-permute-start(bf16[512,160]{0,1:T(8,128)(2,1)S(1)} %convolution_convert_fusion), channel_id=1, source_target_pairs={{0,1},{1,0},{2,3},{3,2},{4,5},{5,4},{6,7},{7,6},{8,9},{9,8},{10,11... | collective-permute-start | bytes 491528 | tf_op jit(solution)/shard_map/ppermute | solution.py:12
  23.1 5.5 %collective-permute-start.1 = (bf16[512]{0:T(512)(128)(2,1)S(1)}, bf16[512]{0:T(512)(128)(2,1)S(1)}, u32[]{:S(2)}, u32[]{:S(2)}) collective-permute-start(bf16[512]{0:T(512)(128)(2,1)S(1)} %get-tuple-element.11), channel_id=1, source_target_pairs={{0,1},{1,0},{2,3},{3,2},{4,5},{5,4},{6,7},{7,6},{8,9},{9,8},{10,11... | collective-permute-start | bytes 3080 | tf_op jit(solution)/shard_map/ppermute | solution.py:12
  25.6 3.4 %collective-permute-start = (bf16[512,160]{0,1:T(8,128)(2,1)S(1)}, bf16[512,160]{0,1:T(8,128)(2,1)S(1)}, u32[]{:S(2)}, u32[]{:S(2)}) collective-permute-start(bf16[512,160]{0,1:T(8,128)(2,1)S(1)} %convolution_convert_fusion.2), channel_id=1, source_target_pairs={{0,1},{1,0},{2,3},{3,2},{4,5},{5,4},{6,7},{7,6},{8,9},{9,8},{10,11... | collective-permute-start | bytes 491528 | tf_op jit(solution)/shard_map/ppermute | solution.py:12
  31.9 5.9 %copy-start.5 = (s32[64]{0:T(128)S(1)}, s32[64]{0:T(128)}, u32[]{:S(2)}) copy-start(s32[64]{0:T(128)} %param.19) | copy-start | bytes 772
  32.0 6.0 %copy-start.4 = (s32[64]{0:T(128)S(1)}, s32[64]{0:T(128)}, u32[]{:S(2)}) copy-start(s32[64]{0:T(128)} %param.18) | copy-start | bytes 772
  32.0 6.0 %copy-start.6 = (s32[64,2]{0,1:T(2,128)S(1)}, s32[64,2]{0,1:T(2,128)}, u32[]{:S(2)}) copy-start(s32[64,2]{0,1:T(2,128)} %param.17) | copy-start | bytes 1540
  33.2 53.2 %all-to-all-start = ((bf16[8,512,160]{1,2,0:T(8,128)(2,1)}), bf16[8,512,160]{1,2,0:T(8,128)(2,1)S(1)}, u32[]{:S(2)}, u32[]{:S(2)}) async-start(bf16[8,512,160]{1,2,0:T(8,128)(2,1)} %broadcast_in_dim.69), calls=%async_computation | async-start | bytes 2621440 | tf_op jit(solution)/shard_map/all_to_all | solution.py:94
  102.7 20.2 %all-to-all-start.1 = ((bf16[64,2,160]{2,1,0:T(2,128)(2,1)}), bf16[64,2,160]{2,1,0:T(2,128)(2,1)S(1)}, u32[]{:S(2)}, u32[]{:S(2)}) async-start(bf16[64,2,160]{2,1,0:T(2,128)(2,1)} %reshape.261), calls=%async_computation.1 | async-start | bytes 131072 | tf_op jit(solution)/shard_map/all_to_all | solution.py:107
  124.0 14.9 %all-to-all-start.2 = ((bf16[64,4,160]{2,1,0:T(4,128)(2,1)}), bf16[64,4,160]{2,1,0:T(4,128)(2,1)S(1)}, u32[]{:S(2)}, u32[]{:S(2)}) async-start(bf16[64,4,160]{2,1,0:T(4,128)(2,1)} %reshape.263), calls=%async_computation.2 | async-start | bytes 262144 | tf_op jit(solution)/shard_map/all_to_all | solution.py:116
Sparse Core Ops, SparseCore 0:
  9.4 83.2 all-gather.1
where the time goes:
time: 147 us
  waiting for transfers between devices  67.3 us (46%)
  starting transfers between devices  32.6 us (22%)
  between operations  21.2 us (14%)
  matrix products  15.1 us (10%)
  local copies, waits for them, and re-layouts  6.95 us (5%)
  other arithmetic  3.64 us (2%)
    all_to_all x1, waiting for transfers between devices, on_device(): gathered = lax.all_to_all(sent, 'head', 0, 0, tiled=True)  44.9 us
    ppermute x3, starting transfers between devices, partner(): lax.ppermute(x, axis, [(i, i ^ 1 << apart) for i in range(lax.axis_size(a...  13.1 us
    all_to_all x1, starting transfers between devices, on_device(): lax.all_to_all(projected.reshape(places, share, width_here), 'tok', 0, 0,...  10.4 us
    all_to_all x1, waiting for transfers between devices, on_device(): lax.all_to_all(projected.reshape(places, share, width_here), 'tok', 0, 0,...  9.7 us
    all_gather x1, waiting for transfers between devices, on_device(): full_weight = lax.all_gather(out_weight, 'head', axis=0, tiled=True)  6.37 us
    all_to_all x1, waiting for transfers between devices, on_device(): lax.all_to_all(pieces.reshape(places, 2 * share, width_here), 'tok', 0, 0...  5.53 us
    dot_general x1, matrix products, on_device(): jnp.einsum('ztf,zfd->td', gathered, full_weight.reshape(group, width_here...  4.83 us
    all_to_all x1, starting transfers between devices, on_device(): gathered = lax.all_to_all(sent, 'head', 0, 0, tiled=True)  4.66 us
  transfers between devices with their start and end apart: 7, of which 4 were waited for; matrix products, arithmetic and copies ran while one was open for 8% of the time, Pallas kernels for 0%

commit v1 on v0

--- a/solution.py
+++ b/solution.py
@@ -46,7 +46,9 @@
     image_offsets,
     owners,
 ):
-    full_weight = lax.all_gather(out_weight, "head", axis=0, tiled=True)
+    full_weight = jnp.concatenate(
+        lax.all_to_all(jnp.stack([out_weight] * lax.axis_size("head")), "head", 0, 0), axis=0
+    )
     block_rows = patches.shape[0]
     width_here = qkv_weight.shape[1]
     heads_here = width_here // HEAD_DIM

time: 147 us -> 193 us (1.31); the launches traced: 147 us -> 191 us
  blocking collectives: 0 us -> 39.3 us
  waiting for transfers between devices: 67.3 us -> 84.3 us
  between operations: 21.2 us -> 7.67 us
    all_to_all x0 -> x1, blocking collectives: none -> 39.3 us  [on_device(): gathered = lax.all_to_all(sent, 'head', 0, 0, tiled=True)]
    all_to_all x1, waiting for transfers between devices: 44.9 us -> 68.9 us  [on_device(): lax.all_to_all(jnp.stack([out_weight] * lax.axis_size('head')), 'head', 0...]
    all_gather x1 -> x0, waiting for transfers between devices: 6.37 us -> none  [on_device(): full_weight = lax.all_gather(out_weight, 'head', axis=0, tiled=True)]
  transfers between devices with their start and end apart: 7 -> 6, of which waited for: 4 -> 3; matrix products, arithmetic and copies ran while one was open for 8% -> 2% of each run, Pallas kernels for 0% -> 0%
where the time goes in v1:
time: 193 us; the launch traced here: 191 us
  waiting for transfers between devices  84.3 us (44%)
  blocking collectives  39.3 us (20%)
  starting transfers between devices  32.8 us (17%)
  matrix products  15.1 us (8%)
  local copies, waits for them, and re-layouts  7.92 us (4%)
  between operations  7.67 us (4%)
  other arithmetic  3.61 us (2%)
    all_to_all x1, waiting for transfers between devices, on_device(): lax.all_to_all(jnp.stack([out_weight] * lax.axis_size('head')), 'head', 0...  68.9 us
    all_to_all x1, blocking collectives, on_device(): gathered = lax.all_to_all(sent, 'head', 0, 0, tiled=True)  39.3 us
    ppermute x3, starting transfers between devices, partner(): lax.ppermute(x, axis, [(i, i ^ 1 << apart) for i in range(lax.axis_size(a...  13.1 us
    all_to_all x1, starting transfers between devices, on_device(): lax.all_to_all(projected.reshape(places, share, width_here), 'tok', 0, 0,...  10.6 us
    all_to_all x1, waiting for transfers between devices, on_device(): lax.all_to_all(projected.reshape(places, share, width_here), 'tok', 0, 0,...  9.7 us
    all_to_all x1, waiting for transfers between devices, on_device(): lax.all_to_all(pieces.reshape(places, 2 * share, width_here), 'tok', 0, 0...  5.7 us
    dot_general x1, matrix products, on_device(): jnp.einsum('ztf,zfd->td', gathered, full_weight.reshape(group, width_here...  4.82 us
    all_to_all x1, starting transfers between devices, on_device(): lax.all_to_all(jnp.stack([out_weight] * lax.axis_size('head')), 'head', 0...  4.57 us
  transfers between devices with their start and end apart: 6, of which 3 were waited for; matrix products, arithmetic and copies ran while one was open for 2% of the time, Pallas kernels for 0%

profile of v1, /device:TPU:1, one launch (start us, length us, event | category | flops | bytes accessed | tf_op | source)
XLA Modules:
  0.0 190.6 jit_solution(17088777241576533101)
XLA Ops:
  0.0 0.0 copy-start
  0.0 0.0 copy-start.3
  0.0 0.8 slice_bitcast_fusion
  0.8 0.8 select_reduce_fusion
  1.6 0.1 fusion.22
  1.7 2.0 %convolution_add_fusion.1 = f32[512,1280]{1,0:T(8,128)S(1)} fusion(bf16[64,1280]{1,0:T(8,128)(2,1)} %param.11, bf16[512,1280]{1,0:T(8,128)(2,1)} %param.10, s32[512]{0:T(512)S(1)} %get-tuple-element.13), kind=kOutput, calls=%fused_computation.3 | convolution fusion | flops 85229568 | bytes 4098048 | tf_op jit(solution)/shard_map/dot_general | solution.py:67
  3.7 0.0 copy-done.3
  3.7 0.6 fusion.41
  4.4 0.0 copy-start.1
  4.4 0.4 multiply_reduce_fusion.1
  4.8 0.0 copy-start.8
  4.8 0.0 copy-start.4
  4.8 0.3 multiply_convert_fusion.1
  5.1 0.8 copy-done.1
  5.9 0.7 copy-done.8
  6.6 0.6 convolution_convert_fusion
  7.2 8.8 %collective-permute-start.2 = (bf16[512,160]{0,1:T(8,128)(2,1)S(1)}, bf16[512,160]{0,1:T(8,128)(2,1)S(1)}, u32[]{:S(2)}, u32[]{:S(2)}) collective-permute-start(bf16[512,160]{0,1:T(8,128)(2,1)S(1)} %convolution_convert_fusion), channel_id=1, source_target_pairs={{0,1},{1,0},{2,3},{3,2},{4,5},{5,4},{6,7},{7,6},{8,9},{9,8},{10,11... | collective-permute-start | bytes 491528 | tf_op jit(solution)/shard_map/ppermute | solution.py:12
  16.0 0.0 copy-done.4
  16.0 1.9 %collective-permute-start.1 = (bf16[512]{0:T(512)(128)(2,1)S(1)}, bf16[512]{0:T(512)(128)(2,1)S(1)}, u32[]{:S(2)}, u32[]{:S(2)}) collective-permute-start(bf16[512]{0:T(512)(128)(2,1)S(1)} %get-tuple-element.11), channel_id=1, source_target_pairs={{0,1},{1,0},{2,3},{3,2},{4,5},{5,4},{6,7},{7,6},{8,9},{9,8},{10,11... | collective-permute-start | bytes 3080 | tf_op jit(solution)/shard_map/ppermute | solution.py:12
  17.9 0.6 convolution_convert_fusion.2
  18.5 2.4 %collective-permute-start = (bf16[512,160]{0,1:T(8,128)(2,1)S(1)}, bf16[512,160]{0,1:T(8,128)(2,1)S(1)}, u32[]{:S(2)}, u32[]{:S(2)}) collective-permute-start(bf16[512,160]{0,1:T(8,128)(2,1)S(1)} %convolution_convert_fusion.2), channel_id=1, source_target_pairs={{0,1},{1,0},{2,3},{3,2},{4,5},{5,4},{6,7},{7,6},{8,9},{9,8},{10,11... | collective-permute-start | bytes 491528 | tf_op jit(solution)/shard_map/ppermute | solution.py:12
  20.9 0.6 convolution_convert_fusion.1
  21.5 0.0 collective-permute-done.1
  21.5 0.4 broadcast_compare_fusion
  21.9 0.0 collective-permute-done.2
  21.9 1.5 fusion
  23.4 0.0 collective-permute-done
  23.5 1.4 fusion.3
  24.8 0.0 copy-start.2
  24.8 0.1 broadcast_in_dim.69
  25.0 39.3 %all_to_all.20 = bf16[8,512,160]{1,2,0:T(8,128)(2,1)S(1)} all-to-all(bf16[8,512,160]{1,2,0:T(8,128)(2,1)S(1)} %broadcast_in_dim.69), channel_id=1, replica_groups=mesh['head'=8,'tok'=64] {'head'}, dimensions={0} | all-to-all | bytes 2621440 | tf_op jit(solution)/shard_map/all_to_all | solution.py:96
  64.3 0.0 copy-done.2
  64.3 1.9 %stack.2 = bf16[8,160,1280]{2,1,0:T(8,128)(2,1)} broadcast(bf16[160,1280]{1,0:T(8,128)(2,1)S(1)} %copy-done.2), dimensions={1,2} | broadcast | bytes 3686400 | tf_op jit(solution)/shard_map/stack | solution.py:50
  66.2 0.0 copy-start.6
  66.2 0.0 copy-start.5
  66.2 0.0 copy-start.7
  66.2 4.6 %all-to-all-start.1 = ((bf16[8,160,1280]{2,1,0:T(8,128)(2,1)}), bf16[8,160,1280]{2,1,0:T(8,128)(2,1)}, u32[]{:S(2)}, u32[]{:S(2)}) async-start(bf16[8,160,1280]{2,1,0:T(8,128)(2,1)} %stack.2), calls=%async_computation.1 | async-start | bytes 6553600 | tf_op jit(solution)/shard_map/all_to_all | solution.py:50
  70.8 0.0 copy-done.6
  70.8 0.1 eq.109
  70.9 0.0 copy-done.5
  70.9 0.0 copy-done.7
  70.9 0.7 fusion.37
  72.9 0.1 copy.12
  74.3 68.9 %all-to-all-done.1 = bf16[8,160,1280]{2,1,0:T(8,128)(2,1)} async-done(((bf16[8,160,1280]{2,1,0:T(8,128)(2,1)}), bf16[8,160,1280]{2,1,0:T(8,128)(2,1)}, u32[]{:S(2)}, u32[]{:S(2)}) %all-to-all-start.1) | async-done | bytes 3276832 | tf_op jit(solution)/shard_map/all_to_all | solution.py:50
  143.2 4.8 %fusion.42 = (f32[512]{0:T(512)S(1)}, f32[512,1280]{1,0:T(8,128)S(1)}) fusion(f32[512,1280]{1,0:T(8,128)} %copy-done.1, bf16[8,512,160]{1,2,0:T(8,128)(2,1)S(1)} %all_to_all.20, bf16[8,160,1280]{2,1,0:T(8,128)(2,1)} %all-to-all-done.1), kind=kOutput, calls=%fused_computation.113 | convolution fusion | flops 1679031808 | bytes 9832448 | tf_op jit(solution)/shard_map/ztf,zfd->td/dot_general | solution.py:97
  148.0 0.4 multiply_reduce_fusion
  148.4 0.3 multiply_convert_fusion
  148.8 1.7 reshape.258
  150.5 0.0 copy-done
  150.5 1.9 convolution_convert_fusion.5
  152.4 0.1 copy.13
  152.5 0.7 reshape.259
  153.2 10.6 %all-to-all-start.2 = ((bf16[64,2,160]{2,1,0:T(2,128)(2,1)}), bf16[64,2,160]{2,1,0:T(2,128)(2,1)S(1)}, u32[]{:S(2)}, u32[]{:S(2)}) async-start(bf16[64,2,160]{2,1,0:T(2,128)(2,1)} %reshape.259), calls=%async_computation.2 | async-start | bytes 131072 | tf_op jit(solution)/shard_map/all_to_all | solution.py:109
  163.8 0.1 fusion.16
  163.9 9.7 %all-to-all-done.2 = bf16[64,2,160]{2,1,0:T(2,128)(2,1)S(1)} async-done(((bf16[64,2,160]{2,1,0:T(2,128)(2,1)}), bf16[64,2,160]{2,1,0:T(2,128)(2,1)S(1)}, u32[]{:S(2)}, u32[]{:S(2)}) %all-to-all-start.2) | async-done | bytes 40992 | tf_op jit(solution)/shard_map/all_to_all | solution.py:109
  173.6 0.1 reshape.260
  173.7 0.2 convolution_convert_fusion.4
  173.9 0.8 reshape.261
  174.7 4.4 %all-to-all-start.3 = ((bf16[64,4,160]{2,1,0:T(4,128)(2,1)}), bf16[64,4,160]{2,1,0:T(4,128)(2,1)S(1)}, u32[]{:S(2)}, u32[]{:S(2)}) async-start(bf16[64,4,160]{2,1,0:T(4,128)(2,1)} %reshape.261), calls=%async_computation.3 | async-start | bytes 262144 | tf_op jit(solution)/shard_map/all_to_all | solution.py:118
  183.9 5.7 %all-to-all-done.3 = bf16[64,4,160]{2,1,0:T(4,128)(2,1)S(1)} async-done(((bf16[64,4,160]{2,1,0:T(4,128)(2,1)}), bf16[64,4,160]{2,1,0:T(4,128)(2,1)S(1)}, u32[]{:S(2)}, u32[]{:S(2)}) %all-to-all-start.3) | async-done | bytes 81952 | tf_op jit(solution)/shard_map/all_to_all | solution.py:118
  189.6 0.1 reshape.262
  189.7 0.9 convolution_convert_fusion.3
  (10 shorter events, 0.1 us)
Async XLA Ops:
  0.0 150.5 %copy-start = (bf16[160,5120]{1,0:T(8,128)(2,1)S(1)}, bf16[160,5120]{1,0:T(8,128)(2,1)}, u32[]{:S(2)}) copy-start(bf16[160,5120]{1,0:T(8,128)(2,1)} %param.15) | copy-start | bytes 4915204
  0.0 3.7 %copy-start.3 = (bf16[64,1280]{1,0:T(8,128)(2,1)S(1)}, bf16[64,1280]{1,0:T(8,128)(2,1)}, u32[]{:S(2)}) copy-start(bf16[64,1280]{1,0:T(8,128)(2,1)} %param.12) | copy-start | bytes 491524
  4.4 1.6 copy-start.1
  4.8 1.8 copy-start.8
  4.8 11.2 %copy-start.4 = (s32[512]{0:T(512)S(1)}, s32[512]{0:T(512)}, u32[]{:S(2)}) copy-start(s32[512]{0:T(512)} %param.16) | copy-start | bytes 6148
  7.2 14.7 %collective-permute-start.2 = (bf16[512,160]{0,1:T(8,128)(2,1)S(1)}, bf16[512,160]{0,1:T(8,128)(2,1)S(1)}, u32[]{:S(2)}, u32[]{:S(2)}) collective-permute-start(bf16[512,160]{0,1:T(8,128)(2,1)S(1)} %convolution_convert_fusion), channel_id=1, source_target_pairs={{0,1},{1,0},{2,3},{3,2},{4,5},{5,4},{6,7},{7,6},{8,9},{9,8},{10,11... | collective-permute-start | bytes 491528 | tf_op jit(solution)/shard_map/ppermute | solution.py:12
  16.0 5.5 %collective-permute-start.1 = (bf16[512]{0:T(512)(128)(2,1)S(1)}, bf16[512]{0:T(512)(128)(2,1)S(1)}, u32[]{:S(2)}, u32[]{:S(2)}) collective-permute-start(bf16[512]{0:T(512)(128)(2,1)S(1)} %get-tuple-element.11), channel_id=1, source_target_pairs={{0,1},{1,0},{2,3},{3,2},{4,5},{5,4},{6,7},{7,6},{8,9},{9,8},{10,11... | collective-permute-start | bytes 3080 | tf_op jit(solution)/shard_map/ppermute | solution.py:12
  18.5 4.9 %collective-permute-start = (bf16[512,160]{0,1:T(8,128)(2,1)S(1)}, bf16[512,160]{0,1:T(8,128)(2,1)S(1)}, u32[]{:S(2)}, u32[]{:S(2)}) collective-permute-start(bf16[512,160]{0,1:T(8,128)(2,1)S(1)} %convolution_convert_fusion.2), channel_id=1, source_target_pairs={{0,1},{1,0},{2,3},{3,2},{4,5},{5,4},{6,7},{7,6},{8,9},{9,8},{10,11... | collective-permute-start | bytes 491528 | tf_op jit(solution)/shard_map/ppermute | solution.py:12
  24.8 39.4 %copy-start.2 = (bf16[160,1280]{1,0:T(8,128)(2,1)S(1)}, bf16[160,1280]{1,0:T(8,128)(2,1)}, u32[]{:S(2)}) copy-start(bf16[160,1280]{1,0:T(8,128)(2,1)} %param.14) | copy-start | bytes 1228804
  66.2 4.6 %copy-start.6 = (s32[64]{0:T(128)S(1)}, s32[64]{0:T(128)}, u32[]{:S(2)}) copy-start(s32[64]{0:T(128)} %param.19) | copy-start | bytes 772
  66.2 4.7 %copy-start.5 = (s32[64]{0:T(128)S(1)}, s32[64]{0:T(128)}, u32[]{:S(2)}) copy-start(s32[64]{0:T(128)} %param.18) | copy-start | bytes 772
  66.2 4.7 %copy-start.7 = (s32[64,2]{0,1:T(2,128)S(1)}, s32[64,2]{0,1:T(2,128)}, u32[]{:S(2)}) copy-start(s32[64,2]{0,1:T(2,128)} %param.17) | copy-start | bytes 1540
  66.2 77.0 %all-to-all-start.1 = ((bf16[8,160,1280]{2,1,0:T(8,128)(2,1)}), bf16[8,160,1280]{2,1,0:T(8,128)(2,1)}, u32[]{:S(2)}, u32[]{:S(2)}) async-start(bf16[8,160,1280]{2,1,0:T(8,128)(2,1)} %stack.2), calls=%async_computation.1 | async-start | bytes 6553600 | tf_op jit(solution)/shard_map/all_to_all | solution.py:50
  153.2 20.4 %all-to-all-start.2 = ((bf16[64,2,160]{2,1,0:T(2,128)(2,1)}), bf16[64,2,160]{2,1,0:T(2,128)(2,1)S(1)}, u32[]{:S(2)}, u32[]{:S(2)}) async-start(bf16[64,2,160]{2,1,0:T(2,128)(2,1)} %reshape.259), calls=%async_computation.2 | async-start | bytes 131072 | tf_op jit(solution)/shard_map/all_to_all | solution.py:109
  174.7 14.9 %all-to-all-start.3 = ((bf16[64,4,160]{2,1,0:T(4,128)(2,1)}), bf16[64,4,160]{2,1,0:T(4,128)(2,1)S(1)}, u32[]{:S(2)}, u32[]{:S(2)}) async-start(bf16[64,4,160]{2,1,0:T(4,128)(2,1)} %reshape.261), calls=%async_computation.3 | async-start | bytes 262144 | tf_op jit(solution)/shard_map/all_to_all | solution.py:118
